TPU v7x, 32 devices: a whole 2x2x4 slice. The times are simulated.
32 devices in a mesh: dp: 16 (over z, y, core), head: 2 (over x).
Axes of the slice: x: 2, y: 2, z: 4, core: 2. Of those that a mesh axis runs over, the one named last changes fastest.
Arguments:
- tokens: bfloat16 [16, 256, 512], P('dp', 'head'), may hold values from -6 to 6
- lengths: int32 [16], P('dp'), may hold values from 32 to 256, as said below
- cotangent: bfloat16 [16, 256, 512], P('dp', 'head'), may hold values from -6 to 6
- glu_weight: bfloat16 [512, 1024], replicated, may hold values from -0.25 to 0.25
- glu_bias: bfloat16 [1024], replicated, may hold values from -1.75 to 1.75
- norm_gain: bfloat16 [4, 512], replicated, may hold values from 0.25 to 1.75
- norm_bias: bfloat16 [4, 512], replicated, may hold values from -1.75 to 1.75
- mid_gain: bfloat16 [2048], replicated, may hold values from 0.25 to 1.75
- mid_bias: bfloat16 [2048], replicated, may hold values from -1.75 to 1.75
- left_weight: bfloat16 [512, 2048], replicated, may hold values from -0.25 to 0.25
- left_bias: bfloat16 [2048], replicated, may hold values from -1.75 to 1.75
- conv_weight: bfloat16 [3, 512, 256], replicated, may hold values from -0.15625 to 0.15625
- conv_bias: bfloat16 [256], replicated, may hold values from -1.75 to 1.75
- depth_weight: bfloat16 [9, 2048], replicated, may hold values from -2 to 2
- point_weight: bfloat16 [2048, 256], replicated, may hold values from -0.125 to 0.125
- point_bias: bfloat16 [256], replicated, may hold values from -1.75 to 1.75
- qkv_weight: bfloat16 [512, 1536], replicated, may hold values from -0.375 to 0.375
- out_weight: bfloat16 [512, 512], replicated, may hold values from -1 to 1
- ffn_in_weight: bfloat16 [512, 2048], replicated, may hold values from -0.25 to 0.25
- ffn_in_bias: bfloat16 [2048], replicated, may hold values from -1.75 to 1.75
- ffn_out_weight: bfloat16 [2048, 512], replicated, may hold values from -0.125 to 0.125
- ffn_out_bias: bfloat16 [512], replicated, may hold values from -1.75 to 1.75
Outputs:
- out_tokens: bfloat16 [16, 256, 512], P('dp', 'head')
- grad_tokens: float32 [16, 256, 512], P('dp', 'head')
- grad_glu_weight: float32 [512, 1024], P('dp')
- grad_glu_bias: float32 [1024], P('dp')
- grad_norm_gain: float32 [4, 512], P(None, 'dp')
- grad_norm_bias: float32 [4, 512], P(None, 'dp')
- grad_mid_gain: float32 [2048], P('dp')
- grad_mid_bias: float32 [2048], P('dp')
- grad_left_weight: float32 [512, 2048], P('dp')
- grad_left_bias: float32 [2048], P('dp')
- grad_conv_weight: float32 [3, 512, 256], P(None, 'dp')
- grad_conv_bias: float32 [256], replicated
- grad_depth_weight: float32 [9, 2048], P(None, 'dp')
- grad_point_weight: float32 [2048, 256], P('dp')
- grad_point_bias: float32 [256], replicated
- grad_qkv_weight: float32 [512, 1536], P('dp')
- grad_out_weight: float32 [512, 512], P('dp')
- grad_ffn_in_weight: float32 [512, 2048], P('dp')
- grad_ffn_in_bias: float32 [2048], P('dp')
- grad_ffn_out_weight: float32 [2048, 512], P('dp')
- grad_ffn_out_bias: float32 [512], P('dp')
Inputs may be any that keep to these rules, and one draw needn't show every extreme that they name: `lengths`: counted from the start of the row; some row is full.
All inputs are finite; a program needn't handle non-finite values.
Results may differ from a plain program's by a relative error of at most 0.03.
The roundings to bfloat16 on the way count: a program that leaves them out, or rounds other values in their place, can miss the bound.
Values may be sent and summed in bfloat16 or wider, within the bound.
No kernel may reach another device: no remote copies, remote signals or barrier semaphores. Data moves between devices by JAX's collectives and lax.ppermute only.
A program may use at most 128 MiB of HBM per device.

v0:
```python
import jax
import jax.numpy as jnp
from jax import lax
from jax.sharding import PartitionSpec as P

HEAD_DIM = 64
EPSILON = 1e-06


def padded(cells, sides, width):
    for axis, dim in sides:
        count = lax.axis_size(axis)
        ends = count - 1
        head = lax.slice_in_dim(cells, 0, width, axis=dim)
        tail = lax.slice_in_dim(cells, cells.shape[dim] - width, cells.shape[dim], axis=dim)
        cells = jnp.concatenate(
            [
                lax.ppermute(tail, axis, [(i, (i + 1) % count) for i in range(ends)]),
                cells,
                lax.ppermute(head, axis, [((i + 1) % count, i) for i in range(ends)]),
            ],
            axis=dim,
        )
    return cells


def layer_norm(inputs, gain_vec, bias_vec):
    average = jnp.mean(inputs, axis=-1, keepdims=True)
    centred = inputs - average
    spread = jnp.mean(centred * centred, axis=-1, keepdims=True)
    return centred * lax.rsqrt(spread + EPSILON) * gain_vec + bias_vec


def project(inputs, weight):
    return jnp.dot(inputs, weight, preferred_element_type=jnp.float32)


def project_back(incoming, weight):
    return jnp.einsum("bte,de->btd", incoming, weight, preferred_element_type=jnp.float32)


def weight_grad(inputs, incoming):
    return jnp.einsum("btd,bte->de", inputs, incoming, preferred_element_type=jnp.float32)


def token_sum(incoming):
    return jnp.sum(incoming.astype(jnp.float32), axis=(0, 1))


def norm_back(inputs, gain_vec, bias_vec, incoming):
    unused, pullback = jax.vjp(layer_norm, inputs, gain_vec, bias_vec)
    return pullback(incoming)


def per_device(
    tokens,
    lengths,
    cotangent,
    glu_weight,
    glu_bias,
    norm_gain,
    norm_bias,
    mid_gain,
    mid_bias,
    left_weight,
    left_bias,
    conv_weight,
    conv_bias,
    depth_weight,
    point_weight,
    point_bias,
    qkv_weight,
    out_weight,
    ffn_in_weight,
    ffn_in_bias,
    ffn_out_weight,
    ffn_out_bias,
):
    row_count, part_len, width = tokens.shape
    groups = lax.axis_size("head")
    seq_len = part_len * groups
    local_width = width // groups
    local_heads = local_width // HEAD_DIM
    half_width = conv_weight.shape[2]
    ffn_width = left_weight.shape[1]
    scale = HEAD_DIM ** (-0.5)
    begin = lax.axis_index("head") * part_len
    places = begin + jnp.arange(part_len, dtype=jnp.int32)
    columns = (places[None, :] < lengths[:, None]).astype(jnp.float32)[:, :, None]
    keys_open = (jnp.arange(seq_len, dtype=jnp.int32)[None, :] < lengths[:, None])[:, None, None, :]
    gains = norm_gain.astype(jnp.float32)
    shifts = norm_bias.astype(jnp.float32)
    mid_gains = mid_gain.astype(jnp.float32)
    mid_shifts = mid_bias.astype(jnp.float32)
    taps = depth_weight.astype(jnp.float32)
    conv_flat = conv_weight.reshape(3 * width, half_width)
    stream_in = tokens.astype(jnp.float32)
    first_norm = layer_norm(stream_in, gains[0], shifts[0]).astype(jnp.bfloat16)
    joined = project(first_norm, glu_weight) + glu_bias.astype(jnp.float32)
    values_part = joined[..., :width]
    gate_part = jax.nn.sigmoid(joined[..., width:])
    after_glu = stream_in + values_part * gate_part
    second_norm = (layer_norm(after_glu, gains[1], shifts[1]) * columns).astype(jnp.bfloat16)
    left_pre = project(second_norm, left_weight) + left_bias.astype(jnp.float32)
    rimmed_second = padded(second_norm, (("head", 1),), 1)
    window = jnp.concatenate(
        [rimmed_second[:, :-2], rimmed_second[:, 1:-1], rimmed_second[:, 2:]], axis=-1
    )
    right_pre = project(window, conv_flat) + conv_bias.astype(jnp.float32)
    combined = jnp.where(left_pre > 0.0, left_pre, 0.0) + jnp.pad(
        jnp.where(right_pre > 0.0, right_pre, 0.0), ((0, 0), (0, 0), (0, ffn_width - half_width))
    )
    third_norm = layer_norm(combined, mid_gains, mid_shifts) * columns
    rimmed_third = padded(third_norm.astype(jnp.bfloat16), (("head", 1),), 4).astype(
        third_norm.dtype
    )
    depthwise = rimmed_third[:, 0:part_len] * taps[0]
    for offset in range(1, 9):
        depthwise = depthwise + rimmed_third[:, offset : offset + part_len] * taps[offset]
    depth_low = depthwise.astype(jnp.bfloat16)
    separable = project(depth_low, point_weight) + point_bias.astype(jnp.float32)
    after_conv = after_glu + jnp.pad(separable, ((0, 0), (0, 0), (0, width - half_width)))
    fourth_norm = layer_norm(after_conv, gains[2], shifts[2]).astype(jnp.bfloat16)
    packed = (
        project(fourth_norm, qkv_weight).astype(jnp.bfloat16).reshape(row_count, part_len, 3, width)
    )
    spread_out = lax.all_to_all(packed, "head", split_axis=3, concat_axis=1, tiled=True)
    shaped = spread_out.reshape(row_count, seq_len, 3, local_heads, HEAD_DIM)
    queries = shaped[:, :, 0]
    keyset = shaped[:, :, 1]
    valueset = shaped[:, :, 2]

    def masked_scores():
        raw_scores = (
            jnp.einsum("bqhd,bkhd->bhqk", queries, keyset, preferred_element_type=jnp.float32)
            * scale
        )
        return jnp.where(keys_open, raw_scores, -1000000000.0)

    scores = masked_scores()
    largest = jnp.max(scores, axis=-1, keepdims=True)
    raised = jnp.exp(scores - largest)
    totals = jnp.sum(raised, axis=-1, keepdims=True)
    log_total = largest + jnp.log(totals)
    context = jnp.einsum(
        "bhqk,bkhd->bqhd",
        (raised / totals).astype(jnp.bfloat16),
        valueset,
        preferred_element_type=jnp.float32,
    )
    context = context.astype(jnp.bfloat16).reshape(row_count, seq_len, local_width)
    returned = lax.all_to_all(context, "head", split_axis=1, concat_axis=2, tiled=True)
    after_attn = after_conv + project(returned, out_weight)
    fifth_norm = layer_norm(after_attn, gains[3], shifts[3]).astype(jnp.bfloat16)
    hidden_pre = project(fifth_norm, ffn_in_weight) + ffn_in_bias.astype(jnp.float32)
    hidden = jnp.where(hidden_pre > 0.0, hidden_pre, 0.0).astype(jnp.bfloat16)
    block_out = after_attn + project(hidden, ffn_out_weight) + ffn_out_bias.astype(jnp.float32)
    grad_stream = cotangent.astype(jnp.float32)
    g_ffn_out = weight_grad(hidden, cotangent)
    g_ffn_out_bias = token_sum(cotangent)
    d_hidden = jnp.where(hidden_pre > 0.0, project_back(cotangent, ffn_out_weight), 0.0).astype(
        jnp.bfloat16
    )
    g_ffn_in = weight_grad(fifth_norm, d_hidden)
    g_ffn_in_bias = token_sum(d_hidden)
    d_fifth, gain_three, shift_three = norm_back(
        after_attn, gains[3], shifts[3], project_back(d_hidden, ffn_in_weight)
    )
    d_after_attn = grad_stream + d_fifth
    d_attn = d_after_attn.astype(jnp.bfloat16)
    g_out = weight_grad(returned, d_attn)
    d_returned = project_back(d_attn, out_weight).astype(jnp.bfloat16)
    d_context = lax.all_to_all(d_returned, "head", split_axis=2, concat_axis=1, tiled=True)
    d_context = d_context.reshape(row_count, seq_len, local_heads, HEAD_DIM)
    probs = jnp.exp(masked_scores() - log_total)
    d_values = jnp.einsum(
        "bhqk,bqhd->bkhd", probs.astype(jnp.bfloat16), d_context, preferred_element_type=jnp.float32
    )
    d_probs = jnp.einsum("bqhd,bkhd->bhqk", d_context, valueset, preferred_element_type=jnp.float32)
    delta = jnp.sum(d_probs * probs, axis=-1, keepdims=True)
    d_scores = (probs * (d_probs - delta)).astype(jnp.bfloat16)
    d_queries = (
        jnp.einsum("bhqk,bkhd->bqhd", d_scores, keyset, preferred_element_type=jnp.float32) * scale
    )
    d_keys = (
        jnp.einsum("bhqk,bqhd->bkhd", d_scores, queries, preferred_element_type=jnp.float32) * scale
    )
    d_spread = jnp.stack([d_queries, d_keys, d_values], axis=2).astype(jnp.bfloat16)
    d_spread = d_spread.reshape(row_count, seq_len, 3, local_width)
    d_packed = lax.all_to_all(d_spread, "head", split_axis=1, concat_axis=3, tiled=True)
    d_packed = d_packed.reshape(row_count, part_len, 3 * width)
    g_qkv = weight_grad(fourth_norm, d_packed)
    upper = (g_ffn_out, g_ffn_out_bias, g_ffn_in, g_ffn_in_bias, g_out, g_qkv)
    d_fourth, gain_two, shift_two = norm_back(
        after_conv, gains[2], shifts[2], project_back(d_packed, qkv_weight)
    )
    d_after_conv = d_after_attn + d_fourth
    d_sep = d_after_conv[..., :half_width].astype(jnp.bfloat16)
    g_point = weight_grad(depth_low, d_sep)
    g_point_bias = token_sum(d_sep)
    d_depth = project_back(d_sep, point_weight)
    g_depth = jnp.stack(
        [
            jnp.sum(d_depth * rimmed_third[:, offset : offset + part_len], axis=(0, 1))
            for offset in range(9)
        ]
    )
    d_rimmed = padded(d_depth.astype(jnp.bfloat16), (("head", 1),), 4).astype(d_depth.dtype)
    d_third = d_rimmed[:, 8 : 8 + part_len] * taps[0]
    for offset in range(1, 9):
        d_third = d_third + d_rimmed[:, 8 - offset : 8 - offset + part_len] * taps[offset]
    d_third = d_third * columns
    d_combined, g_mid_gain, g_mid_bias = norm_back(combined, mid_gains, mid_shifts, d_third)
    d_left = jnp.where(left_pre > 0.0, d_combined, 0.0).astype(jnp.bfloat16)
    d_right = jnp.where(right_pre > 0.0, d_combined[..., :half_width], 0.0).astype(jnp.bfloat16)
    g_left = weight_grad(second_norm, d_left)
    g_left_bias = token_sum(d_left)
    g_conv = weight_grad(window, d_right).reshape(3, width, half_width)
    g_conv_bias = token_sum(d_right)
    d_window = project_back(d_right, conv_flat)
    side_taps = jnp.stack([d_window[..., :width], d_window[..., 2 * width :]], axis=0)
    side_rimmed = padded(side_taps.astype(jnp.bfloat16), (("head", 2),), 1).astype(side_taps.dtype)
    d_second = project_back(d_left, left_weight) + d_window[..., width : 2 * width]
    d_second = d_second + side_rimmed[0][:, 2:] + side_rimmed[1][:, :-2]
    d_second = d_second * columns
    d_norm_one, gain_one, shift_one = norm_back(after_glu, gains[1], shifts[1], d_second)
    d_after_glu = d_after_conv + d_norm_one
    d_values_part = d_after_glu * gate_part
    d_gate_part = d_after_glu * values_part * gate_part * (1.0 - gate_part)
    d_joined = jnp.concatenate([d_values_part, d_gate_part], axis=-1).astype(jnp.bfloat16)
    g_glu = weight_grad(first_norm, d_joined)
    g_glu_bias = token_sum(d_joined)
    d_norm_zero, gain_zero, shift_zero = norm_back(
        stream_in, gains[0], shifts[0], project_back(d_joined, glu_weight)
    )
    grad_input = d_after_glu + d_norm_zero
    g_gains = jnp.stack([gain_zero, gain_one, gain_two, gain_three])
    g_shifts = jnp.stack([shift_zero, shift_one, shift_two, shift_three])
    bias_totals = lax.psum((g_conv_bias, g_point_bias), ("dp", "head"))
    summed = (
        lax.psum_scatter(upper[0], "dp", scatter_dimension=0, tiled=True),
        lax.psum_scatter(upper[1], "dp", scatter_dimension=0, tiled=True),
        lax.psum_scatter(upper[2], "dp", scatter_dimension=0, tiled=True),
        lax.psum_scatter(upper[3], "dp", scatter_dimension=0, tiled=True),
        lax.psum_scatter(upper[4], "dp", scatter_dimension=0, tiled=True),
        lax.psum_scatter(upper[5], "dp", scatter_dimension=0, tiled=True),
        lax.psum_scatter(g_glu, "dp", scatter_dimension=0, tiled=True),
        lax.psum_scatter(g_glu_bias, "dp", scatter_dimension=0, tiled=True),
        lax.psum_scatter(g_gains, "dp", scatter_dimension=1, tiled=True),
        lax.psum_scatter(g_shifts, "dp", scatter_dimension=1, tiled=True),
        lax.psum_scatter(g_mid_gain, "dp", scatter_dimension=0, tiled=True),
        lax.psum_scatter(g_mid_bias, "dp", scatter_dimension=0, tiled=True),
        lax.psum_scatter(g_left, "dp", scatter_dimension=0, tiled=True),
        lax.psum_scatter(g_left_bias, "dp", scatter_dimension=0, tiled=True),
        lax.psum_scatter(g_conv, "dp", scatter_dimension=1, tiled=True),
        lax.psum_scatter(g_depth, "dp", scatter_dimension=1, tiled=True),
        lax.psum_scatter(g_point, "dp", scatter_dimension=0, tiled=True),
    )
    final = (
        lax.psum(summed[0].astype(jnp.bfloat16), "head").astype(jnp.float32),
        lax.psum(summed[1].astype(jnp.bfloat16), "head").astype(jnp.float32),
        lax.psum(summed[2].astype(jnp.bfloat16), "head").astype(jnp.float32),
        lax.psum(summed[3].astype(jnp.bfloat16), "head").astype(jnp.float32),
        lax.psum(summed[4].astype(jnp.bfloat16), "head").astype(jnp.float32),
        lax.psum(summed[5].astype(jnp.bfloat16), "head").astype(jnp.float32),
        lax.psum(summed[6].astype(jnp.bfloat16), "head").astype(jnp.float32),
        lax.psum(summed[7].astype(jnp.bfloat16), "head").astype(jnp.float32),
        lax.psum(summed[8].astype(jnp.bfloat16), "head").astype(jnp.float32),
        lax.psum(summed[9].astype(jnp.bfloat16), "head").astype(jnp.float32),
        lax.psum(summed[10].astype(jnp.bfloat16), "head").astype(jnp.float32),
        lax.psum(summed[11].astype(jnp.bfloat16), "head").astype(jnp.float32),
        lax.psum(summed[12].astype(jnp.bfloat16), "head").astype(jnp.float32),
        lax.psum(summed[13].astype(jnp.bfloat16), "head").astype(jnp.float32),
        lax.psum(summed[14].astype(jnp.bfloat16), "head").astype(jnp.float32),
        lax.psum(summed[15].astype(jnp.bfloat16), "head").astype(jnp.float32),
        lax.psum(summed[16].astype(jnp.bfloat16), "head").astype(jnp.float32),
    )
    return (
        block_out.astype(jnp.bfloat16),
        grad_input,
        final[6],
        final[7],
        final[8],
        final[9],
        final[10],
        final[11],
        final[12],
        final[13],
        final[14],
        bias_totals[0],
        final[15],
        final[16],
        bias_totals[1],
        final[5],
        final[4],
        final[2],
        final[3],
        final[0],
        final[1],
    )


def solution(mesh):
    return jax.shard_map(
        per_device,
        mesh=mesh,
        in_specs=(
            P("dp", "head", None),
            P("dp"),
            P("dp", "head", None),
            P(),
            P(),
            P(),
            P(),
            P(),
            P(),
            P(),
            P(),
            P(),
            P(),
            P(),
            P(),
            P(),
            P(),
            P(),
            P(),
            P(),
            P(),
            P(),
        ),
        out_specs=(
            P("dp", "head", None),
            P("dp", "head", None),
            P("dp", None),
            P("dp"),
            P(None, "dp"),
            P(None, "dp"),
            P("dp"),
            P("dp"),
            P("dp", None),
            P("dp"),
            P(None, "dp", None),
            P(),
            P(None, "dp"),
            P("dp", None),
            P(),
            P("dp", None),
            P("dp", None),
            P("dp", None),
            P("dp"),
            P("dp", None),
            P("dp"),
        ),
        check_vma=False,
    )
```

profile of v0, /device:TPU:0, one launch (start us, length us, event | category | flops | bytes accessed | tf_op | source)
XLA Modules:
  0.0 969.6 jit_solution(5460570614094923607)
XLA Ops:
  17.2 5.0 collective-permute-start
  23.6 4.0 collective-permute-done.1
  33.2 4.1 collective-permute-done.3
  41.5 1.9 copy.94
  43.5 2.1 copy.95
  45.6 4.2 all-to-all-start
  49.8 6.7 all-to-all-done
  58.8 2.0 reshape.963
  62.3 2.1 convolution_convert_fusion.3
  66.0 2.1 reduce.41
  69.6 4.0 all-to-all-start.1
  73.7 4.5 all-to-all-done.1
  83.3 2.1 convolution_add_fusion
  94.0 3.0 reduce.42
  98.6 4.0 all-to-all-start.2
  102.8 4.3 all-to-all-done.2
  122.4 2.0 pad_maximum_fusion
  124.4 9.0 all_to_all.60
  134.2 1.9 copy.110
  136.2 3.0 fusion.65
  140.5 2.1 fusion.35
  144.0 2.5 collective-permute-start.4
  153.7 3.3 multiply_reduce_fusion
  159.6 3.8 collective-permute-start.6
  164.8 4.2 collective-permute-done.7
  176.0 2.1 stack.110
  180.5 2.0 copy.112
  182.4 2.5 fusion.87
  185.3 2.7 fusion.42
  188.1 1.9 fusion.68
  190.1 2.3 fusion.109
  193.5 2.8 fusion.106
  197.5 3.6 fusion.71
  201.1 3.8 fusion.39
  209.2 58.8 %all-reduce.9 = (bf16[1024]{0:T(1024)(128)(2,1)}, bf16[2048]{0:T(1024)(128)(2,1)}, bf16[2048]{0:T(1024)(128)(2,1)}, bf16[2048]{0:T(1024)(128)(2,1)}, bf16[2048]{0:T(1024)(128)(2,1)}, /*index=5*/bf16[512]{0:T(512)(128)(2,1)}) all-reduce(f32[1024]{0:T(1024)S(1)} %convert_reduce_fusion.2, ...), channel_id=3, replica_groups=mesh['dp'=16,'head'=2] {'dp'}, use_global_device_ids=true, to_apply=%region_26.27.clone | all-reduce | flops 9728 | bytes 58368
  277.0 10.3 %reduce-scatter.34.cloned.1.call-done = f32[32,4]{1,0:T(8,128)} async-done(((f32[512,4]{1,0:T(8,128)}), f32[32,4]{1,0:T(8,128)}) %reduce-scatter.34.cloned.1.call-update) | async-done | bytes 528
  288.6 53.8 %reduce-scatter.22.cloned.1.call-done = f32[9,128]{1,0:T(8,128)} async-done(((f32[9,2048]{1,0:T(8,128)}), f32[9,128]{1,0:T(8,128)}) %reduce-scatter.22.cloned.1.call-update) | async-done | bytes 4624 | tf_op jit(solution)/shard_map/reduce_scatter | solution.py:256
  343.7 59.1 %reduce-scatter.28.cloned.1.call-done = f32[32,512]{1,0:T(8,128)} async-done(((f32[512,512]{1,0:T(8,128)}), f32[32,512]{1,0:T(8,128)}) %reduce-scatter.28.cloned.1.call-update) | async-done | bytes 65552 | tf_op jit(solution)/shard_map/reduce_scatter | solution.py:245
  404.2 60.5 %reduce-scatter.20.cloned.1.call-done = f32[3,32,256]{2,1,0:T(8,128)} async-done(((f32[3,512,256]{2,1,0:T(8,128)}), f32[3,32,256]{2,1,0:T(8,128)}) %reduce-scatter.20.cloned.1.call-update) | async-done | bytes 98320 | tf_op jit(solution)/shard_map/reduce_scatter | solution.py:255
  467.0 62.3 %reduce-scatter.24.cloned.1.call-done = f32[128,256]{1,0:T(8,128)} async-done(((f32[2048,256]{1,0:T(8,128)}), f32[128,256]{1,0:T(8,128)}) %reduce-scatter.24.cloned.1.call-update) | async-done | bytes 131088 | tf_op jit(solution)/shard_map/reduce_scatter | solution.py:257
  530.9 62.8 %reduce-scatter.16.cloned.1.call-done = f32[32,1024]{1,0:T(8,128)} async-done(((f32[512,1024]{1,0:T(8,128)}), f32[32,1024]{1,0:T(8,128)}) %reduce-scatter.16.cloned.1.call-update) | async-done | bytes 131088 | tf_op jit(solution)/shard_map/reduce_scatter | solution.py:247
  595.2 68.0 %reduce-scatter.26.cloned.1.call-done = f32[32,1536]{1,0:T(8,128)} async-done(((f32[512,1536]{1,0:T(8,128)}), f32[32,1536]{1,0:T(8,128)}) %reduce-scatter.26.cloned.1.call-update) | async-done | bytes 196624 | tf_op jit(solution)/shard_map/reduce_scatter | solution.py:246
  664.8 74.4 %reduce-scatter.30.cloned.1.call-done = f32[32,2048]{1,0:T(8,128)} async-done(((f32[512,2048]{1,0:T(8,128)}), f32[32,2048]{1,0:T(8,128)}) %reduce-scatter.30.cloned.1.call-update) | async-done | bytes 262160 | tf_op jit(solution)/shard_map/reduce_scatter | solution.py:243
  740.8 73.6 %reduce-scatter.32.cloned.1.call-done = f32[128,512]{1,0:T(8,128)} async-done(((f32[2048,512]{1,0:T(8,128)}), f32[128,512]{1,0:T(8,128)}) %reduce-scatter.32.cloned.1.call-update) | async-done | bytes 262160 | tf_op jit(solution)/shard_map/reduce_scatter | solution.py:241
  816.0 74.6 %reduce-scatter.18.cloned.1.call-done = f32[32,2048]{1,0:T(8,128)} async-done(((f32[512,2048]{1,0:T(8,128)}), f32[32,2048]{1,0:T(8,128)}) %reduce-scatter.18.cloned.1.call-update) | async-done | bytes 262160 | tf_op jit(solution)/shard_map/reduce_scatter | solution.py:253
  894.3 40.0 %all-reduce.8 = (f32[256]{0:T(256)}, f32[256]{0:T(256)}) all-reduce(f32[256]{0:T(256)} %get-tuple-element.67, f32[256]{0:T(256)S(1)} %convert_reduce_fusion.5), channel_id=1, replica_groups=mesh['dp'=16,'head'=2] {'dp','head'}, use_global_device_ids=true, to_apply=%region_54.55 | all-reduce | flops 512 | bytes 4096 | tf_op jit(solution)/shard_map/psum | solution.py:239
  934.9 1.9 add_add_fusion.5
  950.2 3.4 all-reduce.17.cloned.1.call-done
  (439 shorter events, 136.2 us)
Async XLA Ops:
  7.2 78.2 %copy-start = (bf16[2048,512]{1,0:T(8,128)(2,1)S(1)}, bf16[2048,512]{1,0:T(8,128)(2,1)}, u32[]{:S(2)}) copy-start(bf16[2048,512]{1,0:T(8,128)(2,1)} %param.42) | copy-start | bytes 6291460
  7.2 16.3 %copy-start.122 = (bf16[256]{0:T(256)(128)(2,1)S(1)}, bf16[256]{0:T(256)(128)(2,1)}, u32[]{:S(2)}) copy-start(bf16[256]{0:T(256)(128)(2,1)} %param.34) | copy-start | bytes 1540
  7.2 16.3 %copy-start.108 = (bf16[2048]{0:T(1024)(128)(2,1)S(1)}, bf16[2048]{0:T(1024)(128)(2,1)}, u32[]{:S(2)}) copy-start(bf16[2048]{0:T(1024)(128)(2,1)} %param.32) | copy-start | bytes 12292
  7.2 16.3 %copy-start.109 = (bf16[2048]{0:T(1024)(128)(2,1)S(1)}, bf16[2048]{0:T(1024)(128)(2,1)}, u32[]{:S(2)}) copy-start(bf16[2048]{0:T(1024)(128)(2,1)} %param.29) | copy-start | bytes 12292
  7.2 16.3 %copy-start.110 = (bf16[2048]{0:T(1024)(128)(2,1)S(1)}, bf16[2048]{0:T(1024)(128)(2,1)}, u32[]{:S(2)}) copy-start(bf16[2048]{0:T(1024)(128)(2,1)} %param.30) | copy-start | bytes 12292
  7.3 20.4 %copy-start.51 = (bf16[3,512,256]{2,1,0:T(8,128)(2,1)S(1)}, bf16[3,512,256]{2,1,0:T(8,128)(2,1)}, u32[]{:S(2)}) copy-start(bf16[3,512,256]{2,1,0:T(8,128)(2,1)} %param.33) | copy-start | bytes 2359300
  8.5 15.1 %copy-start.71 = (f32[128]{0:T(128)}, f32[128]{0:T(128)S(1)}, u32[]{:S(2)}) copy-start(f32[128]{0:T(128)S(1)} %broadcast_multiply_fusion.4) | copy-start | bytes 1540
  10.1 17.9 %copy-start.80 = (f32[128]{0:T(128)}, f32[128]{0:T(128)S(1)}, u32[]{:S(2)}) copy-start(f32[128]{0:T(128)S(1)} %fusion.93) | copy-start | bytes 1540
  11.5 16.4 %copy-start.68 = (f32[1,512]{1,0:T(1,128)}, f32[1,512]{1,0:T(1,128)S(1)}, u32[]{:S(2)}) copy-start(f32[1,512]{1,0:T(1,128)S(1)} %get-tuple-element.112) | copy-start | bytes 6148
  16.1 22.9 %copy-start.10 = (f32[1,128,512]{2,1,0:T(8,128)}, f32[1,128,512]{2,1,0:T(8,128)S(1)}, u32[]{:S(2)}) copy-start(f32[1,128,512]{2,1,0:T(8,128)S(1)} %get-tuple-element.86) | copy-start | bytes 786436
  16.1 13.1 %copy-start.100 = (f32[128]{0:T(128)}, f32[128]{0:T(128)S(1)}, u32[]{:S(2)}) copy-start(f32[128]{0:T(128)S(1)} %broadcast_multiply_fusion.3) | copy-start | bytes 1540
  17.0 11.6 %copy-start.37 = (bf16[512,2048]{1,0:T(8,128)(2,1)S(1)}, bf16[512,2048]{1,0:T(8,128)(2,1)}, u32[]{:S(2)}) copy-start(bf16[512,2048]{1,0:T(8,128)(2,1)} %param.31) | copy-start | bytes 6291460
  17.0 12.6 %copy-start.102 = (f32[128]{0:T(128)}, f32[128]{0:T(128)S(1)}, u32[]{:S(2)}) copy-start(f32[128]{0:T(128)S(1)} %compare_convert_fusion) | copy-start | bytes 1540
  17.2 12.1 %copy-start.43 = (bf16[1,128,512]{2,1,0:T(8,128)(2,1)}, bf16[1,128,512]{2,1,0:T(8,128)(2,1)S(1)}, u32[]{:S(2)}) copy-start(bf16[1,128,512]{2,1,0:T(8,128)(2,1)S(1)} %multiply_convert_fusion.4) | copy-start | bytes 393220
  17.2 6.4 collective-permute-start
  22.2 5.5 collective-permute-start.1
  30.0 3.1 collective-permute-start.2
  31.7 5.6 collective-permute-start.3
  39.5 99.6 %copy-start.85 = (f32[128]{0:T(128)}, f32[128]{0:T(128)S(1)}, u32[]{:S(2)}) copy-start(f32[128]{0:T(128)S(1)} %broadcast_multiply_fusion.2) | copy-start | bytes 1540
  39.7 99.5 %copy-start.96 = (f32[128]{0:T(128)}, f32[128]{0:T(128)S(1)}, u32[]{:S(2)}) copy-start(f32[128]{0:T(128)S(1)} %fusion.96) | copy-start | bytes 1540
  45.6 10.9 %all-to-all-start = ((bf16[1,128,3,512]{1,2,0,3:T(4,128)(2,1)}), bf16[1,128,3,512]{1,2,0,3:T(4,128)(2,1)}, u32[]{:S(2)}, u32[]{:S(2)}) async-start(bf16[1,128,3,512]{1,2,0,3:T(4,128)(2,1)} %copy.95), calls=%async_computation | async-start | bytes 1048576 | tf_op jit(solution)/shard_map/all_to_all | solution.py:127
  62.3 11.4 %copy-start.111 = (bf16[2048]{0:T(1024)(128)(2,1)S(1)}, bf16[2048]{0:T(1024)(128)(2,1)}, u32[]{:S(2)}) copy-start(bf16[2048]{0:T(1024)(128)(2,1)} %param.41) | copy-start | bytes 12292
  64.4 18.9 %copy-start.66 = (f32[1,512]{1,0:T(1,128)S(1)}, f32[1,512]{1,0:T(1,128)}, u32[]{:S(2)}) copy-start(f32[1,512]{1,0:T(1,128)} %get-tuple-element.110) | copy-start | bytes 6148
  64.4 18.9 %copy-start.76 = (f32[1,512]{1,0:T(1,128)S(1)}, f32[1,512]{1,0:T(1,128)}, u32[]{:S(2)}) copy-start(f32[1,512]{1,0:T(1,128)} %get-tuple-element.114) | copy-start | bytes 6148
  69.6 8.6 all-to-all-start.1
  98.6 8.6 all-to-all-start.2
  102.6 173.1 %reduce-scatter.36.cloned.1.call-start = ((), (), s32[]{:S(2)}) async-start(), calls=%async_computation.25 | async-start | bytes 278528
  142.6 11.1 %copy-start.27 = (f32[1,128,256]{2,1,0:T(8,128)S(1)}, f32[1,128,256]{2,1,0:T(8,128)}, u32[]{:S(2)}) copy-start(f32[1,128,256]{2,1,0:T(8,128)} %copy-done.26) | copy-start | bytes 393220
  144.0 7.0 collective-permute-start.4
  146.5 5.9 collective-permute-start.5
  159.6 5.1 collective-permute-start.6
  163.4 5.5 collective-permute-start.7
  170.6 17.5 %copy-start.34 = (bf16[1,128,512]{2,1,0:T(8,128)(2,1)}, bf16[1,128,512]{2,1,0:T(8,128)(2,1)S(1)}, u32[]{:S(2)}) copy-start(bf16[1,128,512]{2,1,0:T(8,128)(2,1)S(1)} %get-tuple-element.72) | copy-start | bytes 393220
  170.8 17.3 %copy-start.35 = (bf16[1,128,512]{2,1,0:T(8,128)(2,1)}, bf16[1,128,512]{2,1,0:T(8,128)(2,1)S(1)}, u32[]{:S(2)}) copy-start(bf16[1,128,512]{2,1,0:T(8,128)(2,1)S(1)} %multiply_convert_fusion.2) | copy-start | bytes 393220
  173.5 113.7 %reduce-scatter.34.cloned.1.call-start = ((), (), s32[]{:S(2)}) async-start(), calls=%async_computation.24 | async-start | bytes 278528
  175.9 166.5 %reduce-scatter.22.cloned.1.call-start = ((), (), s32[]{:S(2)}) async-start(), calls=%async_computation.18 | async-start | bytes 139264 | tf_op jit(solution)/shard_map/reduce_scatter | solution.py:256
  178.2 224.6 %reduce-scatter.28.cloned.1.call-start = ((), (), s32[]{:S(2)}) async-start(), calls=%async_computation.21 | async-start | bytes 1114112 | tf_op jit(solution)/shard_map/reduce_scatter | solution.py:245
  179.6 285.2 %reduce-scatter.20.cloned.1.call-start = ((), (), s32[]{:S(2)}) async-start(), calls=%async_computation.17 | async-start | bytes 1671168 | tf_op jit(solution)/shard_map/reduce_scatter | solution.py:255
  185.0 344.4 %reduce-scatter.24.cloned.1.call-start = ((), (), s32[]{:S(2)}) async-start(), calls=%async_computation.19 | async-start | bytes 2228224 | tf_op jit(solution)/shard_map/reduce_scatter | solution.py:257
  188.0 405.7 %reduce-scatter.16.cloned.1.call-start = ((), (), s32[]{:S(2)}) async-start(), calls=%async_computation.15 | async-start | bytes 2228224 | tf_op jit(solution)/shard_map/reduce_scatter | solution.py:247
  190.0 473.2 %reduce-scatter.26.cloned.1.call-start = ((), (), s32[]{:S(2)}) async-start(), calls=%async_computation.20 | async-start | bytes 3342336 | tf_op jit(solution)/shard_map/reduce_scatter | solution.py:246
  192.4 546.7 %reduce-scatter.30.cloned.1.call-start = ((), (), s32[]{:S(2)}) async-start(), calls=%async_computation.22 | async-start | bytes 4456448 | tf_op jit(solution)/shard_map/reduce_scatter | solution.py:243
  196.3 618.1 %reduce-scatter.32.cloned.1.call-start = ((), (), s32[]{:S(2)}) async-start(), calls=%async_computation.23 | async-start | bytes 4456448 | tf_op jit(solution)/shard_map/reduce_scatter | solution.py:241
  201.1 689.5 %reduce-scatter.18.cloned.1.call-start = ((), (), s32[]{:S(2)}) async-start(), calls=%async_computation.16 | async-start | bytes 4456448 | tf_op jit(solution)/shard_map/reduce_scatter | solution.py:253
  205.0 731.8 %all-reduce.15.cloned.1.call-start = ((), (), s32[]{:S(2)}) async-start(), calls=%async_computation.26 | async-start | bytes 182272 | tf_op jit(solution)/shard_map/psum | solution.py:267
  466.3 487.3 %all-reduce.17.cloned.1.call-start = ((), (), s32[]{:S(2)}) async-start(), calls=%async_computation.27 | async-start | bytes 1245184 | tf_op jit(solution)/shard_map/psum | solution.py:266
  892.2 42.7 %copy-start.73 = (f32[128]{0:T(128)S(1)}, f32[128]{0:T(128)}, u32[]{:S(2)}) copy-start(f32[128]{0:T(128)} %copy-done.71) | copy-start | bytes 1540
  892.2 42.7 %copy-start.82 = (f32[128]{0:T(128)S(1)}, f32[128]{0:T(128)}, u32[]{:S(2)}) copy-start(f32[128]{0:T(128)} %copy-done.80) | copy-start | bytes 1540
  (101 other events, 388.4 us)
Sparse Core Ops, SparseCore 0:
  173.7 55.6 reduce-scatter.35
  232.9 54.3 reduce-scatter.33
  291.2 51.1 reduce-scatter.21
  346.3 56.4 reduce-scatter.27
  406.3 58.3 reduce-scatter.19
  468.8 60.5 reduce-scatter.23
  533.1 60.5 reduce-scatter.15
  598.0 65.1 reduce-scatter.25
  667.6 71.5 reduce-scatter.29
  742.9 71.4 reduce-scatter.31
  818.7 71.8 reduce-scatter.17
  895.1 21.7 all-reduce.14
  921.3 32.2 all-reduce.16
where the time goes:
time: 973 us; the launch traced here: 970 us
  waiting for transfers between devices  632 us (65%)
  blocking collectives  108 us (11%)
  other arithmetic  68.7 us (7%)
  local copies, waits for them, and re-layouts  62.2 us (6%)
  matrix products  48.9 us (5%)
  starting transfers between devices  31.3 us (3%)
  between operations  18.4 us (2%)
    reduce_scatter x1, waiting for transfers between devices, per_device(): lax.psum_scatter(g_left, 'dp', scatter_dimension=0, tiled=True)  74.6 us
    reduce_scatter x1, waiting for transfers between devices, per_device(): lax.psum_scatter(upper[2], 'dp', scatter_dimension=0, tiled=True)  74.4 us
    reduce_scatter x1, waiting for transfers between devices, per_device(): lax.psum_scatter(upper[0], 'dp', scatter_dimension=0, tiled=True)  73.6 us
    reduce_scatter x1, waiting for transfers between devices, per_device(): lax.psum_scatter(upper[5], 'dp', scatter_dimension=0, tiled=True)  68 us
    reduce_scatter x1, waiting for transfers between devices, per_device(): lax.psum_scatter(g_glu, 'dp', scatter_dimension=0, tiled=True)  62.8 us
    reduce_scatter x1, waiting for transfers between devices, per_device(): lax.psum_scatter(g_point, 'dp', scatter_dimension=0, tiled=True)  62.3 us
    reduce_scatter x1, waiting for transfers between devices, per_device(): lax.psum_scatter(g_conv, 'dp', scatter_dimension=1, tiled=True)  60.5 us
    reduce_scatter x1, waiting for transfers between devices, per_device(): lax.psum_scatter(upper[4], 'dp', scatter_dimension=0, tiled=True)  59.1 us
  transfers between devices with their start and end apart: 24, of which 18 were waited for; matrix products, arithmetic and copies ran while one was open for 8% of the time, Pallas kernels for 0%

commit v1 on v0

--- a/solution.py
+++ b/solution.py
@@ -236,7 +236,9 @@
     grad_input = d_after_glu + d_norm_zero
     g_gains = jnp.stack([gain_zero, gain_one, gain_two, gain_three])
     g_shifts = jnp.stack([shift_zero, shift_one, shift_two, shift_three])
-    bias_totals = lax.psum((g_conv_bias, g_point_bias), ("dp", "head"))
+    bias_totals = (g_conv_bias, g_point_bias)
+    for over in ("dp", "head"):
+        bias_totals = lax.psum(bias_totals, over)
     summed = (
         lax.psum_scatter(upper[0], "dp", scatter_dimension=0, tiled=True),
         lax.psum_scatter(upper[1], "dp", scatter_dimension=0, tiled=True),

time: 973 us -> 972 us (level)
  blocking collectives: 108 us -> 73.4 us
  waiting for transfers between devices: 632 us -> 665 us
    psum x1, blocking collectives: 40 us -> 5.61 us  [per_device(): bias_totals = lax.psum(bias_totals, over)]
    psum x1, waiting for transfers between devices: 3.4 us -> 22.6 us  [per_device(): lax.psum(summed[6].astype(jnp.bfloat16), 'head').astype(jnp.float32)]
    psum x1, waiting for transfers between devices: 0.01 us -> 15.5 us  [per_device(): lax.psum(summed[7].astype(jnp.bfloat16), 'head').astype(jnp.float32)]
  transfers between devices with their start and end apart: 24 -> 24, of which waited for: 18 -> 19; matrix products, arithmetic and copies ran while one was open for 8% -> 8% of each run, Pallas kernels for 0% -> 0%
where the time goes in v1:
time: 972 us; the launch traced here: 969 us
  waiting for transfers between devices  665 us (68%)
  blocking collectives  73.4 us (8%)
  other arithmetic  69.4 us (7%)
  local copies, waits for them, and re-layouts  62.3 us (6%)
  matrix products  48.9 us (5%)
  starting transfers between devices  31.3 us (3%)
  between operations  18.4 us (2%)
    reduce_scatter x1, waiting for transfers between devices, per_device(): lax.psum_scatter(g_left, 'dp', scatter_dimension=0, tiled=True)  74.3 us
    reduce_scatter x1, waiting for transfers between devices, per_device(): lax.psum_scatter(upper[2], 'dp', scatter_dimension=0, tiled=True)  74.2 us
    reduce_scatter x1, waiting for transfers between devices, per_device(): lax.psum_scatter(upper[0], 'dp', scatter_dimension=0, tiled=True)  73.4 us
    reduce_scatter x1, waiting for transfers between devices, per_device(): lax.psum_scatter(upper[5], 'dp', scatter_dimension=0, tiled=True)  68 us
    reduce_scatter x1, waiting for transfers between devices, per_device(): lax.psum_scatter(g_glu, 'dp', scatter_dimension=0, tiled=True)  62.9 us
    reduce_scatter x1, waiting for transfers between devices, per_device(): lax.psum_scatter(g_point, 'dp', scatter_dimension=0, tiled=True)  62.4 us
    reduce_scatter x1, waiting for transfers between devices, per_device(): lax.psum_scatter(g_conv, 'dp', scatter_dimension=1, tiled=True)  60.6 us
    reduce_scatter x1, waiting for transfers between devices, per_device(): lax.psum_scatter(upper[4], 'dp', scatter_dimension=0, tiled=True)  59.1 us
  transfers between devices with their start and end apart: 24, of which 19 were waited for; matrix products, arithmetic and copies ran while one was open for 8% of the time, Pallas kernels for 0%

profile of v1, /device:TPU:0, one launch (start us, length us, event | category | flops | bytes accessed | tf_op | source)
XLA Modules:
  0.0 968.7 jit_solution(4105749904012410108)
XLA Ops:
  17.2 5.0 collective-permute-start
  23.6 4.0 collective-permute-done.1
  33.2 4.1 collective-permute-done.3
  41.5 1.9 copy.94
  43.5 2.1 copy.95
  45.6 4.2 all-to-all-start
  49.9 6.7 all-to-all-done
  58.8 2.0 reshape.963
  62.3 2.1 convolution_convert_fusion.3
  66.0 2.1 reduce.41
  69.7 4.0 all-to-all-start.1
  73.7 4.5 all-to-all-done.1
  83.3 2.1 convolution_add_fusion
  94.0 3.0 reduce.42
  98.6 4.0 all-to-all-start.2
  102.8 4.3 all-to-all-done.2
  122.5 2.0 pad_maximum_fusion
  124.5 9.0 all_to_all.60
  134.3 1.9 copy.110
  136.2 3.0 fusion.65
  140.5 2.1 fusion.35
  144.0 2.5 collective-permute-start.4
  153.7 3.3 multiply_reduce_fusion
  159.7 3.8 collective-permute-start.6
  164.8 4.2 collective-permute-done.7
  176.0 2.1 stack.110
  180.5 2.0 copy.112
  182.4 2.5 fusion.87
  185.3 2.7 fusion.42
  190.1 2.3 fusion.109
  193.5 2.8 fusion.106
  197.5 3.6 fusion.71
  201.2 3.8 fusion.39
  210.7 58.8 %all-reduce.8 = (bf16[1024]{0:T(1024)(128)(2,1)}, bf16[2048]{0:T(1024)(128)(2,1)}, bf16[2048]{0:T(1024)(128)(2,1)}, bf16[2048]{0:T(1024)(128)(2,1)}, f32[256]{0:...) all-reduce(f32[1024]{0:T(1024)S(1)} %convert_reduce_fusion.2, ...), channel_id=3, replica_groups=mesh['dp'=16,'head'=2] {'dp'}, use_global_device_ids=true, to_apply=%region_26.27.clone | all-reduce | flops 10240 | bytes 62464
  278.6 8.6 reduce-scatter.34.cloned.1.call-done
  288.6 53.9 %reduce-scatter.22.cloned.1.call-done = f32[9,128]{1,0:T(8,128)} async-done(((f32[9,2048]{1,0:T(8,128)}), f32[9,128]{1,0:T(8,128)}) %reduce-scatter.22.cloned.1.call-update) | async-done | bytes 4624 | tf_op jit(solution)/shard_map/reduce_scatter | solution.py:258
  343.7 59.1 %reduce-scatter.28.cloned.1.call-done = f32[32,512]{1,0:T(8,128)} async-done(((f32[512,512]{1,0:T(8,128)}), f32[32,512]{1,0:T(8,128)}) %reduce-scatter.28.cloned.1.call-update) | async-done | bytes 65552 | tf_op jit(solution)/shard_map/reduce_scatter | solution.py:247
  404.3 60.6 %reduce-scatter.20.cloned.1.call-done = f32[3,32,256]{2,1,0:T(8,128)} async-done(((f32[3,512,256]{2,1,0:T(8,128)}), f32[3,32,256]{2,1,0:T(8,128)}) %reduce-scatter.20.cloned.1.call-update) | async-done | bytes 98320 | tf_op jit(solution)/shard_map/reduce_scatter | solution.py:257
  467.1 62.4 %reduce-scatter.24.cloned.1.call-done = f32[128,256]{1,0:T(8,128)} async-done(((f32[2048,256]{1,0:T(8,128)}), f32[128,256]{1,0:T(8,128)}) %reduce-scatter.24.cloned.1.call-update) | async-done | bytes 131088 | tf_op jit(solution)/shard_map/reduce_scatter | solution.py:259
  531.0 62.9 %reduce-scatter.16.cloned.1.call-done = f32[32,1024]{1,0:T(8,128)} async-done(((f32[512,1024]{1,0:T(8,128)}), f32[32,1024]{1,0:T(8,128)}) %reduce-scatter.16.cloned.1.call-update) | async-done | bytes 131088 | tf_op jit(solution)/shard_map/reduce_scatter | solution.py:249
  595.4 68.0 %reduce-scatter.26.cloned.1.call-done = f32[32,1536]{1,0:T(8,128)} async-done(((f32[512,1536]{1,0:T(8,128)}), f32[32,1536]{1,0:T(8,128)}) %reduce-scatter.26.cloned.1.call-update) | async-done | bytes 196624 | tf_op jit(solution)/shard_map/reduce_scatter | solution.py:248
  665.0 74.2 %reduce-scatter.30.cloned.1.call-done = f32[32,2048]{1,0:T(8,128)} async-done(((f32[512,2048]{1,0:T(8,128)}), f32[32,2048]{1,0:T(8,128)}) %reduce-scatter.30.cloned.1.call-update) | async-done | bytes 262160 | tf_op jit(solution)/shard_map/reduce_scatter | solution.py:245
  740.8 73.4 %reduce-scatter.32.cloned.1.call-done = f32[128,512]{1,0:T(8,128)} async-done(((f32[2048,512]{1,0:T(8,128)}), f32[128,512]{1,0:T(8,128)}) %reduce-scatter.32.cloned.1.call-update) | async-done | bytes 262160 | tf_op jit(solution)/shard_map/reduce_scatter | solution.py:243
  815.9 74.3 %reduce-scatter.18.cloned.1.call-done = f32[32,2048]{1,0:T(8,128)} async-done(((f32[512,2048]{1,0:T(8,128)}), f32[32,2048]{1,0:T(8,128)}) %reduce-scatter.18.cloned.1.call-update) | async-done | bytes 262160 | tf_op jit(solution)/shard_map/reduce_scatter | solution.py:255
  892.9 5.6 all-reduce.9
  899.2 1.9 add_add_fusion.5
  901.1 15.5 %all-reduce.15.cloned.1.call-done = (bf16[64]{0:T(256)(128)(2,1)}, bf16[4,32]{1,0:T(4,128)(2,1)}, bf16[4,32]{1,0:T(4,128)(2,1)}, bf16[128]{0:T(256)(128)(2,1)}, ...) async-done(((bf16[64]{0:T(256)(128)(2,1)}, ...) | async-done | bytes 85968 | tf_op jit(solution)/shard_map/psum | solution.py:269
  930.0 22.6 %all-reduce.17.cloned.1.call-done = (bf16[32,1024]{1,0:T(8,128)(2,1)}, bf16[32,2048]{1,0:T(8,128)(2,1)}, bf16[128,256]{1,0:T(8,128)(2,1)}, bf16[32,1536]{1,0:T(8...) async-done(((bf16[32,1024]{1,0:T(8,128)(2,1)}, bf16[32,2048]{1,0:T(8,128)(2,1)}, bf16[128,256]{1,0:T(8,128)(2,1)}, bf16[32,1536]{1,0:T(8,128)(2,1)}, ...) | async-done | bytes 622608 | tf_op jit(solution)/shard_map/psum | solution.py:268
  (439 shorter events, 138.8 us)
Async XLA Ops:
  7.2 78.2 %copy-start = (bf16[2048,512]{1,0:T(8,128)(2,1)S(1)}, bf16[2048,512]{1,0:T(8,128)(2,1)}, u32[]{:S(2)}) copy-start(bf16[2048,512]{1,0:T(8,128)(2,1)} %param.42) | copy-start | bytes 6291460
  7.2 16.3 %copy-start.122 = (bf16[256]{0:T(256)(128)(2,1)S(1)}, bf16[256]{0:T(256)(128)(2,1)}, u32[]{:S(2)}) copy-start(bf16[256]{0:T(256)(128)(2,1)} %param.34) | copy-start | bytes 1540
  7.2 16.3 %copy-start.108 = (bf16[2048]{0:T(1024)(128)(2,1)S(1)}, bf16[2048]{0:T(1024)(128)(2,1)}, u32[]{:S(2)}) copy-start(bf16[2048]{0:T(1024)(128)(2,1)} %param.32) | copy-start | bytes 12292
  7.2 16.3 %copy-start.109 = (bf16[2048]{0:T(1024)(128)(2,1)S(1)}, bf16[2048]{0:T(1024)(128)(2,1)}, u32[]{:S(2)}) copy-start(bf16[2048]{0:T(1024)(128)(2,1)} %param.29) | copy-start | bytes 12292
  7.2 16.3 %copy-start.110 = (bf16[2048]{0:T(1024)(128)(2,1)S(1)}, bf16[2048]{0:T(1024)(128)(2,1)}, u32[]{:S(2)}) copy-start(bf16[2048]{0:T(1024)(128)(2,1)} %param.30) | copy-start | bytes 12292
  7.3 20.4 %copy-start.51 = (bf16[3,512,256]{2,1,0:T(8,128)(2,1)S(1)}, bf16[3,512,256]{2,1,0:T(8,128)(2,1)}, u32[]{:S(2)}) copy-start(bf16[3,512,256]{2,1,0:T(8,128)(2,1)} %param.33) | copy-start | bytes 2359300
  8.5 15.1 %copy-start.71 = (f32[128]{0:T(128)}, f32[128]{0:T(128)S(1)}, u32[]{:S(2)}) copy-start(f32[128]{0:T(128)S(1)} %broadcast_multiply_fusion.4) | copy-start | bytes 1540
  10.1 17.9 %copy-start.80 = (f32[128]{0:T(128)}, f32[128]{0:T(128)S(1)}, u32[]{:S(2)}) copy-start(f32[128]{0:T(128)S(1)} %fusion.93) | copy-start | bytes 1540
  11.5 16.4 %copy-start.68 = (f32[1,512]{1,0:T(1,128)}, f32[1,512]{1,0:T(1,128)S(1)}, u32[]{:S(2)}) copy-start(f32[1,512]{1,0:T(1,128)S(1)} %get-tuple-element.114) | copy-start | bytes 6148
  16.1 23.0 %copy-start.10 = (f32[1,128,512]{2,1,0:T(8,128)}, f32[1,128,512]{2,1,0:T(8,128)S(1)}, u32[]{:S(2)}) copy-start(f32[1,128,512]{2,1,0:T(8,128)S(1)} %get-tuple-element.88) | copy-start | bytes 786436
  16.1 13.1 %copy-start.100 = (f32[128]{0:T(128)}, f32[128]{0:T(128)S(1)}, u32[]{:S(2)}) copy-start(f32[128]{0:T(128)S(1)} %broadcast_multiply_fusion.3) | copy-start | bytes 1540
  17.0 11.6 %copy-start.37 = (bf16[512,2048]{1,0:T(8,128)(2,1)S(1)}, bf16[512,2048]{1,0:T(8,128)(2,1)}, u32[]{:S(2)}) copy-start(bf16[512,2048]{1,0:T(8,128)(2,1)} %param.31) | copy-start | bytes 6291460
  17.0 12.6 %copy-start.102 = (f32[128]{0:T(128)}, f32[128]{0:T(128)S(1)}, u32[]{:S(2)}) copy-start(f32[128]{0:T(128)S(1)} %compare_convert_fusion) | copy-start | bytes 1540
  17.2 12.1 %copy-start.43 = (bf16[1,128,512]{2,1,0:T(8,128)(2,1)}, bf16[1,128,512]{2,1,0:T(8,128)(2,1)S(1)}, u32[]{:S(2)}) copy-start(bf16[1,128,512]{2,1,0:T(8,128)(2,1)S(1)} %multiply_convert_fusion.4) | copy-start | bytes 393220
  17.2 6.4 collective-permute-start
  22.2 5.5 collective-permute-start.1
  30.0 3.2 collective-permute-start.2
  31.7 5.6 collective-permute-start.3
  39.6 99.6 %copy-start.85 = (f32[128]{0:T(128)}, f32[128]{0:T(128)S(1)}, u32[]{:S(2)}) copy-start(f32[128]{0:T(128)S(1)} %broadcast_multiply_fusion.2) | copy-start | bytes 1540
  39.7 99.5 %copy-start.96 = (f32[128]{0:T(128)}, f32[128]{0:T(128)S(1)}, u32[]{:S(2)}) copy-start(f32[128]{0:T(128)S(1)} %fusion.96) | copy-start | bytes 1540
  45.6 10.9 %all-to-all-start = ((bf16[1,128,3,512]{1,2,0,3:T(4,128)(2,1)}), bf16[1,128,3,512]{1,2,0,3:T(4,128)(2,1)}, u32[]{:S(2)}, u32[]{:S(2)}) async-start(bf16[1,128,3,512]{1,2,0,3:T(4,128)(2,1)} %copy.95), calls=%async_computation | async-start | bytes 1048576 | tf_op jit(solution)/shard_map/all_to_all | solution.py:127
  62.3 11.4 %copy-start.111 = (bf16[2048]{0:T(1024)(128)(2,1)S(1)}, bf16[2048]{0:T(1024)(128)(2,1)}, u32[]{:S(2)}) copy-start(bf16[2048]{0:T(1024)(128)(2,1)} %param.41) | copy-start | bytes 12292
  64.4 18.9 %copy-start.66 = (f32[1,512]{1,0:T(1,128)S(1)}, f32[1,512]{1,0:T(1,128)}, u32[]{:S(2)}) copy-start(f32[1,512]{1,0:T(1,128)} %get-tuple-element.112) | copy-start | bytes 6148
  64.4 18.9 %copy-start.76 = (f32[1,512]{1,0:T(1,128)S(1)}, f32[1,512]{1,0:T(1,128)}, u32[]{:S(2)}) copy-start(f32[1,512]{1,0:T(1,128)} %get-tuple-element.116) | copy-start | bytes 6148
  69.7 8.6 all-to-all-start.1
  98.6 8.6 all-to-all-start.2
  102.6 174.6 %reduce-scatter.36.cloned.1.call-start = ((), (), s32[]{:S(2)}) async-start(), calls=%async_computation.25 | async-start | bytes 278528
  142.6 11.1 %copy-start.2 = (f32[128,2048]{1,0:T(8,128)S(1)}, f32[128,2048]{1,0:T(8,128)}, u32[]{:S(2)}) copy-start(f32[128,2048]{1,0:T(8,128)} %copy-done.1) | copy-start | bytes 3145732
  142.6 11.1 %copy-start.27 = (f32[1,128,256]{2,1,0:T(8,128)S(1)}, f32[1,128,256]{2,1,0:T(8,128)}, u32[]{:S(2)}) copy-start(f32[1,128,256]{2,1,0:T(8,128)} %copy-done.26) | copy-start | bytes 393220
  144.0 7.0 collective-permute-start.4
  146.5 5.9 collective-permute-start.5
  158.5 10.6 %copy-start.20 = (bf16[1,128,2048]{2,1,0:T(8,128)(2,1)}, bf16[1,128,2048]{2,1,0:T(8,128)(2,1)S(1)}, u32[]{:S(2)}) copy-start(bf16[1,128,2048]{2,1,0:T(8,128)(2,1)S(1)} %get-tuple-element.72) | copy-start | bytes 1572868
  159.7 5.1 collective-permute-start.6
  163.4 5.5 collective-permute-start.7
  170.6 17.5 %copy-start.34 = (bf16[1,128,512]{2,1,0:T(8,128)(2,1)}, bf16[1,128,512]{2,1,0:T(8,128)(2,1)S(1)}, u32[]{:S(2)}) copy-start(bf16[1,128,512]{2,1,0:T(8,128)(2,1)S(1)} %get-tuple-element.74) | copy-start | bytes 393220
  170.8 17.3 %copy-start.35 = (bf16[1,128,512]{2,1,0:T(8,128)(2,1)}, bf16[1,128,512]{2,1,0:T(8,128)(2,1)S(1)}, u32[]{:S(2)}) copy-start(bf16[1,128,512]{2,1,0:T(8,128)(2,1)S(1)} %multiply_convert_fusion.2) | copy-start | bytes 393220
  173.6 113.7 %reduce-scatter.34.cloned.1.call-start = ((), (), s32[]{:S(2)}) async-start(), calls=%async_computation.24 | async-start | bytes 278528
  175.9 166.5 %reduce-scatter.22.cloned.1.call-start = ((), (), s32[]{:S(2)}) async-start(), calls=%async_computation.18 | async-start | bytes 139264 | tf_op jit(solution)/shard_map/reduce_scatter | solution.py:258
  178.2 224.6 %reduce-scatter.28.cloned.1.call-start = ((), (), s32[]{:S(2)}) async-start(), calls=%async_computation.21 | async-start | bytes 1114112 | tf_op jit(solution)/shard_map/reduce_scatter | solution.py:247
  179.6 285.3 %reduce-scatter.20.cloned.1.call-start = ((), (), s32[]{:S(2)}) async-start(), calls=%async_computation.17 | async-start | bytes 1671168 | tf_op jit(solution)/shard_map/reduce_scatter | solution.py:257
  185.0 344.5 %reduce-scatter.24.cloned.1.call-start = ((), (), s32[]{:S(2)}) async-start(), calls=%async_computation.19 | async-start | bytes 2228224 | tf_op jit(solution)/shard_map/reduce_scatter | solution.py:259
  188.0 405.9 %reduce-scatter.16.cloned.1.call-start = ((), (), s32[]{:S(2)}) async-start(), calls=%async_computation.15 | async-start | bytes 2228224 | tf_op jit(solution)/shard_map/reduce_scatter | solution.py:249
  190.0 473.4 %reduce-scatter.26.cloned.1.call-start = ((), (), s32[]{:S(2)}) async-start(), calls=%async_computation.20 | async-start | bytes 3342336 | tf_op jit(solution)/shard_map/reduce_scatter | solution.py:248
  192.5 546.7 %reduce-scatter.30.cloned.1.call-start = ((), (), s32[]{:S(2)}) async-start(), calls=%async_computation.22 | async-start | bytes 4456448 | tf_op jit(solution)/shard_map/reduce_scatter | solution.py:245
  196.3 618.0 %reduce-scatter.32.cloned.1.call-start = ((), (), s32[]{:S(2)}) async-start(), calls=%async_computation.23 | async-start | bytes 4456448 | tf_op jit(solution)/shard_map/reduce_scatter | solution.py:243
  201.1 689.1 %reduce-scatter.18.cloned.1.call-start = ((), (), s32[]{:S(2)}) async-start(), calls=%async_computation.16 | async-start | bytes 4456448 | tf_op jit(solution)/shard_map/reduce_scatter | solution.py:255
  205.0 711.6 %all-reduce.15.cloned.1.call-start = ((), (), s32[]{:S(2)}) async-start(), calls=%async_computation.26 | async-start | bytes 182272 | tf_op jit(solution)/shard_map/psum | solution.py:269
  466.4 486.3 %all-reduce.17.cloned.1.call-start = ((), (), s32[]{:S(2)}) async-start(), calls=%async_computation.27 | async-start | bytes 1245184 | tf_op jit(solution)/shard_map/psum | solution.py:268
  (101 other events, 383.1 us)
Sparse Core Ops, SparseCore 0:
  173.7 55.5 reduce-scatter.35
  232.8 54.3 reduce-scatter.33
  291.2 51.2 reduce-scatter.21
  346.4 56.4 reduce-scatter.27
  406.3 58.4 reduce-scatter.19
  468.9 60.5 reduce-scatter.23
  533.2 60.5 reduce-scatter.15
  598.2 65.1 reduce-scatter.25
  667.8 71.3 reduce-scatter.29
  742.9 71.3 reduce-scatter.31
  818.6 71.5 reduce-scatter.17
  894.7 21.8 all-reduce.14
  920.9 31.6 all-reduce.16
